TPU v7x, 256 devices: a whole 4x4x8 slice. The times are simulated.
256 devices in a mesh: leaf: 32 (over z, x), rhs: 8 (over y, core).
Axes of the slice: x: 4, y: 4, z: 8, core: 2. Of those that a mesh axis runs over, the one named last changes fastest.
Arguments:
- charges: float32 [24576, 8192], P('leaf', 'rhs'), parts along dimension 1, may hold values from -6 to 6
- near_blocks: float32 [32, 3, 768, 768], P('leaf'), may hold values from -0.125 to 0.125
- neighbours: int32 [32, 2], P('leaf'), may hold values from 0 to 31, as said below
- compress: float32 [32, 768, 192], P('leaf'), may hold values from -0.21875 to 0.21875
- transfer: float32 [32, 5, 2, 192, 192], P('leaf'), may hold values from -0.3125 to 0.3125
- expand: float32 [32, 768, 192], P('leaf'), may hold values from -0.4375 to 0.4375
Outputs:
- potential: float32 [24576, 8192], P('leaf', 'rhs'), parts along dimension 1
There are 8 independent parts, one for each index of `rhs`. A program takes and returns all parts, laid end to end along the dimension named above; an argument that names none is the same for every part. Nothing has to cross between parts.
Inputs may be any that keep to these rules, and one draw needn't show every extreme that they name: `neighbours`: row i lists two different leaves, each of (i - 2), (i - 1), (i + 1), (i + 2) modulo 32; never i itself.
All inputs are finite; a program needn't handle non-finite values.
Results may differ from a plain program's by a relative error of at most 0.0001.
Values sent between devices are 32-bit elements; how exact they have to be, the bound alone decides.
A program may use at most 128 MiB of HBM per device.

v0:
```python
import jax
import jax.numpy as jnp
from jax import lax
from jax.sharding import PartitionSpec as P


def partner(shard, axis, distance):
    return lax.ppermute(shard, axis, [(i, i ^ 1 << distance) for i in range(lax.axis_size(axis))])


def passed_along(value, axis, steps):
    count = lax.axis_size(axis)
    pairs = [(source, (source + steps) % count) for source in range(count)]
    return lax.ppermute(value, axis, pairs)


def pick_block(offset, pieces):
    chosen = jnp.zeros_like(pieces[1])
    for step in (-2, -1, 1, 2):
        chosen = jnp.where(offset == step, pieces[step], chosen)
    return chosen


def fine_sweep(coeffs, transfer, level_count):
    hi = lax.Precision.HIGHEST
    for level in range(level_count):
        partner_coeffs = partner(coeffs, "leaf", level)
        coeffs = jnp.dot(transfer[0, level, 0], coeffs, precision=hi) + jnp.dot(
            transfer[0, level, 1], partner_coeffs, precision=hi
        )
    return coeffs


def per_device(charges, near_blocks, neighbours, compress, transfer, expand):
    hi = lax.Precision.HIGHEST
    count = lax.axis_size("leaf")
    here = lax.axis_index("leaf")
    pieces = {}
    for step in (1, -1):
        pieces[step] = passed_along(charges, "leaf", -step)
    for step in (1, -1):
        pieces[2 * step] = passed_along(pieces[step], "leaf", -step)
    offsets = (neighbours[0] - here) % count
    offsets = jnp.where(offsets > count // 2, offsets - count, offsets)
    coeffs = jnp.einsum("ar,ac->rc", compress[0], charges, precision=hi)
    levels = count.bit_length() - 1
    coeffs = fine_sweep(coeffs, transfer, levels)
    near = jnp.dot(near_blocks[0, 0], charges, precision=hi)
    near = near + jnp.dot(near_blocks[0, 1], pick_block(offsets[0], pieces), precision=hi)
    near = near + jnp.dot(near_blocks[0, 2], pick_block(offsets[1], pieces), precision=hi)
    far = jnp.dot(expand[0], coeffs, precision=hi)
    return near + far


def solution(mesh):
    in_specs = (
        P("leaf", "rhs"),
        P("leaf", None, None, None),
        P("leaf", None),
        P("leaf", None, None),
        P("leaf", None, None, None, None),
        P("leaf", None, None),
    )
    out_specs = P("leaf", "rhs")
    return jax.shard_map(
        per_device, mesh=mesh, in_specs=in_specs, out_specs=out_specs, check_vma=False
    )
```

profile of v0, /device:TPU:16, one launch (start us, length us, event | category | flops | bytes accessed | tf_op | source)
XLA Modules:
  0.0 286.6 jit_solution(16431438086976504623)
XLA Ops:
  0.0 0.0 copy-start
  0.0 0.0 copy-start.2
  0.0 8.1 %collective-permute-start = (f32[768,1024]{1,0:T(8,128)}, f32[768,1024]{1,0:T(8,128)}, u32[]{:S(2)}, u32[]{:S(2)}) collective-permute-start(f32[768,1024]{1,0:T(8,128)} %param.6), channel_id=1, source_target_pairs={{0,248},{8,0},{16,8},{24,16},{32,24},{40,32},{48,40},{56,48},{64,5... | collective-permute-start | bytes 9437192 | tf_op jit(solution)/shard_map/ppermute | solution.py:14
  8.1 0.0 collective-permute-start.2
  8.1 4.3 %fusion.33 = f32[192,1024]{1,0:T(8,128)S(1)} fusion(f32[768,1024]{1,0:T(8,128)} %param.6, f32[1,768,192]{1,2,0:T(8,128)} %param.9), kind=kOutput, calls=%fused_computation.37 | convolution fusion | flops 1811939328 | bytes 4521984 | tf_op jit(solution)/shard_map/ar,ac->rc/dot_general | solution.py:45
  12.3 0.1 collective-permute-start.4
  12.4 0.0 copy-done.2
  12.5 0.8 fusion.48
  13.3 79.2 %collective-permute-done.4 = f32[192,1024]{1,0:T(8,128)S(1)} collective-permute-done((f32[192,1024]{1,0:T(8,128)S(1)}, f32[192,1024]{1,0:T(8,128)S(1)}, u32[]{:S(2)}, u32[]{:S(2)}) %collective-permute-start.4) | collective-permute-done | bytes 786464 | tf_op jit(solution)/shard_map/ppermute | solution.py:8
  92.5 0.8 convolution_add_fusion.4
  93.4 0.1 collective-permute-start.5
  93.5 0.8 fusion.45
  94.3 0.0 copy-start.3
  94.3 19.0 %collective-permute-done.5 = f32[192,1024]{1,0:T(8,128)S(1)} collective-permute-done((f32[192,1024]{1,0:T(8,128)S(1)}, f32[192,1024]{1,0:T(8,128)S(1)}, u32[]{:S(2)}, u32[]{:S(2)}) %collective-permute-start.5) | collective-permute-done | bytes 786464 | tf_op jit(solution)/shard_map/ppermute | solution.py:8
  113.4 0.8 convolution_add_fusion.3
  114.2 0.1 collective-permute-start.6
  114.3 0.0 collective-permute-done
  114.3 3.7 %collective-permute-start.1 = (f32[768,1024]{1,0:T(8,128)}, f32[768,1024]{1,0:T(8,128)}, u32[]{:S(2)}, u32[]{:S(2)}) collective-permute-start(f32[768,1024]{1,0:T(8,128)} %collective-permute-done), channel_id=1, source_target_pairs={{0,248},{8,0},{16,8},{24,16},{32,24},{40,32},{48,40},{56,48},{64,5... | collective-permute-start | bytes 9437192 | tf_op jit(solution)/shard_map/ppermute | solution.py:14
  118.0 0.0 collective-permute-done.2
  118.0 0.0 collective-permute-start.3
  118.0 0.8 fusion.42
  118.9 15.9 %collective-permute-done.6 = f32[192,1024]{1,0:T(8,128)S(1)} collective-permute-done((f32[192,1024]{1,0:T(8,128)S(1)}, f32[192,1024]{1,0:T(8,128)S(1)}, u32[]{:S(2)}, u32[]{:S(2)}) %collective-permute-start.6) | collective-permute-done | bytes 786464 | tf_op jit(solution)/shard_map/ppermute | solution.py:8
  134.8 0.8 convolution_add_fusion.2
  135.6 0.1 collective-permute-start.7
  135.8 0.0 copy-done.3
  135.8 0.0 copy-start.1
  135.8 0.8 fusion.39
  136.6 99.7 %collective-permute-done.7 = f32[192,1024]{1,0:T(8,128)} collective-permute-done((f32[192,1024]{1,0:T(8,128)S(1)}, f32[192,1024]{1,0:T(8,128)}, u32[]{:S(2)}, u32[]{:S(2)}) %collective-permute-start.7) | collective-permute-done | bytes 786464 | tf_op jit(solution)/shard_map/ppermute | solution.py:8
  236.3 2.0 convolution_add_fusion.1
  238.3 2.1 collective-permute-start.8
  240.4 0.6 fusion.63
  245.9 0.0 copy-done.1
  245.9 0.0 slice-start
  245.9 9.5 %fusion.12 = f32[768,1024]{1,0:T(8,128)S(1)} fusion(f32[768,1024]{1,0:T(8,128)S(1)} %copy-done.1, f32[1,3,768,768]{3,2,1,0:T(8,128)} %param.7), kind=kOutput, calls=%fused_computation.15 | convolution fusion | flops 7247757312 | bytes 8650752 | tf_op jit(solution)/shard_map/dot_general | solution.py:48
  255.4 0.0 slice-start.1
  255.5 1.8 fusion.36
  257.3 4.0 %collective-permute-done.8 = f32[192,1024]{1,0:T(8,128)S(1)} collective-permute-done((f32[192,1024]{1,0:T(8,128)S(1)}, f32[192,1024]{1,0:T(8,128)S(1)}, u32[]{:S(2)}, u32[]{:S(2)}) %collective-permute-start.8) | collective-permute-done | bytes 786464 | tf_op jit(solution)/shard_map/ppermute | solution.py:8
  261.3 1.8 convolution_add_fusion
  263.1 0.0 copy-done
  263.1 3.0 %fusion.31 = f32[1024,768]{0,1:T(8,128)S(1)} fusion(f32[1024,192]{1,0:T(8,128)S(1)} %convolution_add_fusion, f32[1,768,192]{1,2,0:T(8,128)S(1)} %copy-done), kind=kOutput, calls=%fused_computation.35 | convolution fusion | flops 1811939328 | bytes 4521984 | tf_op jit(solution)/shard_map/dot_general | solution.py:51
  266.1 0.0 collective-permute-done.1
  266.1 0.0 collective-permute-done.3
  266.1 0.0 slice-done
  266.1 0.0 slice-done.1
  266.1 9.7 %fusion.5 = f32[1024,768]{0,1:T(8,128)S(1)} fusion(f32[768,1024]{1,0:T(8,128)} %collective-permute-done.1, f32[768,1024]{1,0:T(8,128)} %collective-permute-done, f32[768,1024]{1,0:T(8,128)} %collective-permute-done.2, f32[768,1024]{1,0:T(8,128)} %collective-permute-done.3, f32[1,3,768,768]{3,2,1,0:T(8,128)S(1)} %bitcast.85, pred[]{:T(512)} %bitcast.5, ...), kind=kOutput, calls=%fused_computation.8 | convolution fusion | flops 7250903040 | bytes 18087940 | tf_op jit(solution)/shard_map/dot_general | solution.py:49
  275.9 10.7 %bitcast_add_fusion = f32[768,1024]{1,0:T(8,128)} fusion(f32[1024,768]{0,1:T(8,128)S(1)} %fusion.31, f32[768,1024]{1,0:T(8,128)S(1)} %fusion.12, f32[1024,768]{0,1:T(8,128)S(1)} %fusion.5, f32[1,3,768,768]{3,2,1,0:T(8,128)S(1)} %bitcast.85, f32[768,1024]{1,0:T(8,128)} %collective-permute-done.1, f32[768,1024]{1,0:T(8,128)} %collective-permute-done, ...), kind=kOutput, calls=%fused_computation | convolution fusion | flops 7253262336 | bytes 27525124 | tf_op jit(solution)/shard_map/dot_general | solution.py:50
  (2 shorter events, 0.0 us)
Async XLA Ops:
  0.0 263.1 %copy-start = (f32[1,768,192]{1,2,0:T(8,128)S(1)}, f32[1,768,192]{1,2,0:T(8,128)}, u32[]{:S(2)}) copy-start(f32[1,768,192]{1,2,0:T(8,128)} %param.11) | copy-start | bytes 1769476
  0.0 12.4 %copy-start.2 = (f32[1,5,2,192,192]{4,3,2,1,0:T(8,128)S(1)}, f32[1,5,2,192,192]{4,3,2,1,0:T(8,128)}, u32[]{:S(2)}) copy-start(f32[1,5,2,192,192]{4,3,2,1,0:T(8,128)} %param.10) | copy-start | bytes 4423684
  0.0 114.3 %collective-permute-start = (f32[768,1024]{1,0:T(8,128)}, f32[768,1024]{1,0:T(8,128)}, u32[]{:S(2)}, u32[]{:S(2)}) collective-permute-start(f32[768,1024]{1,0:T(8,128)} %param.6), channel_id=1, source_target_pairs={{0,248},{8,0},{16,8},{24,16},{32,24},{40,32},{48,40},{56,48},{64,5... | collective-permute-start | bytes 9437192 | tf_op jit(solution)/shard_map/ppermute | solution.py:14
  8.1 109.9 %collective-permute-start.2 = (f32[768,1024]{1,0:T(8,128)}, f32[768,1024]{1,0:T(8,128)}, u32[]{:S(2)}, u32[]{:S(2)}) collective-permute-start(f32[768,1024]{1,0:T(8,128)} %param.6), channel_id=1, source_target_pairs={{0,8},{8,16},{16,24},{24,32},{32,40},{40,48},{48,56},{56,64},{64,7... | collective-permute-start | bytes 9437192 | tf_op jit(solution)/shard_map/ppermute | solution.py:14
  12.3 80.2 %collective-permute-start.4 = (f32[192,1024]{1,0:T(8,128)S(1)}, f32[192,1024]{1,0:T(8,128)S(1)}, u32[]{:S(2)}, u32[]{:S(2)}) collective-permute-start(f32[192,1024]{1,0:T(8,128)S(1)} %fusion.33), channel_id=1, source_target_pairs={{0,8},{8,0},{16,24},{24,16},{32,40},{40,32},{48,56},{56,48},{64,72... | collective-permute-start | bytes 2359304 | tf_op jit(solution)/shard_map/ppermute | solution.py:8
  93.4 20.0 %collective-permute-start.5 = (f32[192,1024]{1,0:T(8,128)S(1)}, f32[192,1024]{1,0:T(8,128)S(1)}, u32[]{:S(2)}, u32[]{:S(2)}) collective-permute-start(f32[192,1024]{1,0:T(8,128)S(1)} %bitcast.88), channel_id=1, source_target_pairs={{0,16},{8,24},{16,0},{24,8},{32,48},{40,56},{48,32},{56,40},{64,80... | collective-permute-start | bytes 2359304 | tf_op jit(solution)/shard_map/ppermute | solution.py:8
  94.3 41.4 %copy-start.3 = (s32[1,2]{1,0:T(1,128)S(1)}, s32[1,2]{1,0:T(1,128)}, u32[]{:S(2)}) copy-start(s32[1,2]{1,0:T(1,128)} %param.8) | copy-start | bytes 28
  114.2 20.6 %collective-permute-start.6 = (f32[192,1024]{1,0:T(8,128)S(1)}, f32[192,1024]{1,0:T(8,128)S(1)}, u32[]{:S(2)}, u32[]{:S(2)}) collective-permute-start(f32[192,1024]{1,0:T(8,128)S(1)} %bitcast.86), channel_id=1, source_target_pairs={{0,32},{8,40},{16,48},{24,56},{32,0},{40,8},{48,16},{56,24},{64,96... | collective-permute-start | bytes 2359304 | tf_op jit(solution)/shard_map/ppermute | solution.py:8
  114.3 151.8 %collective-permute-start.1 = (f32[768,1024]{1,0:T(8,128)}, f32[768,1024]{1,0:T(8,128)}, u32[]{:S(2)}, u32[]{:S(2)}) collective-permute-start(f32[768,1024]{1,0:T(8,128)} %collective-permute-done), channel_id=1, source_target_pairs={{0,248},{8,0},{16,8},{24,16},{32,24},{40,32},{48,40},{56,48},{64,5... | collective-permute-start | bytes 9437192 | tf_op jit(solution)/shard_map/ppermute | solution.py:14
  118.0 148.1 %collective-permute-start.3 = (f32[768,1024]{1,0:T(8,128)}, f32[768,1024]{1,0:T(8,128)}, u32[]{:S(2)}, u32[]{:S(2)}) collective-permute-start(f32[768,1024]{1,0:T(8,128)} %collective-permute-done.2), channel_id=1, source_target_pairs={{0,8},{8,16},{16,24},{24,32},{32,40},{40,48},{48,56},{56,64},{64,7... | collective-permute-start | bytes 9437192 | tf_op jit(solution)/shard_map/ppermute | solution.py:14
  135.6 100.7 %collective-permute-start.7 = (f32[192,1024]{1,0:T(8,128)S(1)}, f32[192,1024]{1,0:T(8,128)}, u32[]{:S(2)}, u32[]{:S(2)}) collective-permute-start(f32[192,1024]{1,0:T(8,128)S(1)} %bitcast.87), channel_id=1, source_target_pairs={{0,64},{8,72},{16,80},{24,88},{32,96},{40,104},{48,112},{56,120},{... | collective-permute-start | bytes 2359304 | tf_op jit(solution)/shard_map/ppermute | solution.py:8
  135.8 110.2 %copy-start.1 = (f32[768,1024]{1,0:T(8,128)S(1)}, f32[768,1024]{1,0:T(8,128)}, u32[]{:S(2)}) copy-start(f32[768,1024]{1,0:T(8,128)} %param.6) | copy-start | bytes 9437188
  238.3 23.0 %collective-permute-start.8 = (f32[192,1024]{1,0:T(8,128)S(1)}, f32[192,1024]{1,0:T(8,128)S(1)}, u32[]{:S(2)}, u32[]{:S(2)}) collective-permute-start(f32[192,1024]{1,0:T(8,128)S(1)} %bitcast.89), channel_id=1, source_target_pairs={{0,128},{8,136},{16,144},{24,152},{32,160},{40,168},{48,176},{56,1... | collective-permute-start | bytes 2359304 | tf_op jit(solution)/shard_map/ppermute | solution.py:8
  245.9 20.2 %slice-start = ((s8[7077888]{0:T(1024)(128)(4,1)}), s8[4194304]{0:T(1024)(128)(4,1)S(1)}, s32[]{:S(2)}) async-start(s8[7077888]{0:T(1024)(128)(4,1)} %bitcast.84), calls=%async_computation | async-start | bytes 8388608
  255.4 10.7 %slice-start.1 = ((s8[7077888]{0:T(1024)(128)(4,1)}), s8[2883584]{0:T(1024)(128)(4,1)S(1)}, s32[]{:S(2)}) async-start(s8[7077888]{0:T(1024)(128)(4,1)} %bitcast.84), calls=%async_computation.1 | async-start | bytes 5767168
where the time goes:
time: 287 us
  waiting for transfers between devices  218 us (76%)
  matrix products  48.7 us (17%)
  starting transfers between devices  14.2 us (5%)
  between operations  5.17 us (2%)
    ppermute x5, waiting for transfers between devices, partner(): lax.ppermute(shard, axis, [(i, i ^ 1 << distance) for i in range(lax.axis...  218 us
    ppermute x4, starting transfers between devices, passed_along(): return lax.ppermute(value, axis, pairs)  11.7 us
    dot_general x1, matrix products, per_device(): jnp.dot(near_blocks[0, 2], pick_block(offsets[1], pieces), precision=hi)  10.7 us
    dot_general x1, matrix products, per_device(): jnp.dot(near_blocks[0, 1], pick_block(offsets[0], pieces), precision=hi)  9.72 us
    dot_general x1, matrix products, per_device(): near = jnp.dot(near_blocks[0, 0], charges, precision=hi)  9.49 us
    dot_general x5, matrix products, fine_sweep(): jnp.dot(transfer[0, level, 1], partner_coeffs, precision=hi)  6.34 us
  transfers between devices with their start and end apart: 9, of which 5 were waited for; matrix products, arithmetic and copies ran while one was open for 10% of the time, Pallas kernels for 0%

commit v1 on v0

v1 whole, which is shorter than its diff:
```python
import functools

import jax
import jax.numpy as jnp
from jax import lax
from jax.experimental import pallas as pl
from jax.experimental.pallas import tpu as pltpu
from jax.sharding import PartitionSpec as P

F32, BF16 = jnp.float32, jnp.bfloat16
XS = 4
PARTS = 4
ROUNDS = 6
COUNT = {"P": 2, "Q": 4}
SLOTS = (("A1", "P", 4), ("A1", "Q", 2), ("A2", "P", 2), ("A2", "Q", 4), ("A3", "P", 4),
         ("A3", "Q", 2), ("ZR", "P", 2), ("ZR", "Q", 4), ("Z0", "Q", 4))
BASE, HOLD = {}, 0
for _slot, _link, _count in SLOTS:
    BASE[_slot, _link] = HOLD
    HOLD += _count
OTHER = {"P": "Q", "Q": "P"}
PLUS = {-2: 0, -1: 1, 1: 2, 2: 3}
OWN = 4
RELAYED = (0, 2)

ORDER = (
    "own Q 0", "comp 0", "prep 4", "comp 1", "prep 0", "L 0 0", "L 0 1", "own Q 1", "Z0 0",
    "prep 2", "comp 3", "comp 2", "L 1 1", "ownmm 0", "L 0 3", "prep 1", "own P 0", "Z0 1",
    "L 2 1", "L 0 2", "L 1 0", "own Q 2", "L 2 0", "ownmm 1", "prep 3", "L 1 3", "A1 Q 0", "L 3 1",
    "A1 P 0", "L 2 3", "L 1 2", "own P 1", "Z0 2", "A2 P 0", "A1 P 1", "own Q 3", "L 2 2",
    "A1 P 2", "A2 Q 0", "Z0 3", "L 3 0", "A1 Q 1", "ZR Q 0", "A2 Q 1", "L 3 2", "ZR P 0", "A2 Q 2",
    "A1 P 3", "A3 Q 0", "ZR Q 1", "A2 P 1", "R 0", "R 2", "A3 P 0", "A2 Q 3", "ZR Q 2", "A3 P 1",
    "L 3 3", "ZR P 1", "ZR Q 3", "L 4 2", "A3 P 2", "L 4 1", "L 4 0", "A3 P 3", "A3 Q 1", "L 4 3",
)


def tokens():
    for token in ORDER:
        name, *args = token.split()
        yield name, args


def split(value):
    high = value.astype(BF16)
    return high, (value - high.astype(F32)).astype(BF16)


def three(value):
    high, low = split(value)
    return jnp.concatenate([high, low, high], axis=0)


def matmul(left, right):
    return jnp.dot(left, right, preferred_element_type=F32)


def kernel(zs, nb, x_hbm, near_hbm, compress_hbm, transfer_hbm, expand_hbm, out,
           xv, x_high, x_low, got, w_high, w_low, near, comp, comp3, trans, trans6,
           expa, expa3, sent, came, mid, load_sem, near_send, near_recv, far_send, far_recv,
           mid_send, mid_recv):
    rows, cols = out.shape
    tall, wide = rows // ROUNDS, cols // PARTS
    rank = comp3.shape[0]
    leaf, r = lax.axis_index("leaf"), lax.axis_index("rhs")
    x, z = leaf % XS, leaf // XS
    odd = x % 2
    step = {"P": 1 - 2 * odd, "Q": 2 * odd - 1}
    end = jnp.logical_or(x == 0, x == XS - 1)
    middle = jnp.logical_not(end)

    def chip(dx, dz):
        return ((z + dz + zs) % zs) * XS + (x + dx + XS) % XS, r

    def partner(level):
        bit = (leaf // 2**level) % 2
        return leaf + (1 - 2 * bit) * 2**level, r

    def load(i, src, dst):
        return pltpu.make_async_copy(src, dst, load_sem.at[i])

    loads = {
        "comp": load(0, compress_hbm, comp),
        "x": load(1, x_hbm, xv),
        "trans": load(2, transfer_hbm, trans),
        "near": load(3, near_hbm, near),
        "expa": load(4, expand_hbm, expa),
    }
    for item in loads.values():
        item.start()

    barrier = pltpu.get_barrier_semaphore()
    greeted = [chip(1, 0), chip(-1, 0), partner(1), chip(0, 1), chip(0, -1), chip(0, 2),
               chip(0, -2), partner(4)]
    for device in greeted:
        pl.semaphore_signal(barrier, inc=1, device_id=device, device_id_type=pl.DeviceIdType.MESH)
    pl.semaphore_wait(barrier, len(greeted))

    def remote(src, dst, send, recv, device):
        return pltpu.make_async_remote_copy(
            src_ref=src, dst_ref=dst, send_sem=send, recv_sem=recv,
            device_id=device, device_id_type=pl.DeviceIdType.MESH)

    def near_copy(send, src, slot, link, m, device):
        at = BASE[slot, link] + m
        return remote(src, got.at[at], near_send.at[send], near_recv.at[at], device)

    def own_rows(link, m):
        first = jnp.where(step[link] == 1, 0, ROUNDS - COUNT[link])
        return x_hbm.at[pl.ds(pl.multiple_of(tall * (first + m), tall), tall)]

    def own_copy(link, m):
        return near_copy(HOLD + m + 4 * (link == "P"), own_rows(link, m), "A1", OTHER[link], m,
                         chip(step[link], 0))

    def lift_copy(m):
        return near_copy(HOLD + m, own_rows("Q", m), "Z0", "Q", m, chip(0, step["Q"]))

    def pass_copy(slot, link, m):
        source = BASE[slot, link] + m
        to = {"Z0": "A1", "A1": "A2", "A2": "A3", "ZR": "A3"}[slot]
        send = BASE["A3", OTHER[link]] + m if to == "A3" else source
        return near_copy(send, got.at[source], to, OTHER[link], m, chip(step[link], 0))

    def z_copy(link, m):
        h = jnp.where(step[link] == 1, 0, 1)
        wraps = x == (XS - 1) * h
        dz = jnp.where(wraps, 1, -1) * step[link]
        source = BASE["A2", link] + m
        return near_copy(source, got.at[source], "ZR", link, m, chip(0, dz))

    def arrived(slot, link, m):
        at = BASE[slot, link] + m
        remote(got.at[at], got.at[at], near_send.at[at], near_recv.at[at], chip(1, 0)).wait_recv()

    def weight_of(slot, link):
        h = jnp.where(step[link] == 1, 0, 1)
        if slot == "A1":
            return 1 + h
        if slot == "A3":
            return 2 - h
        wraps = x == (XS - 1) * h
        ahead, behind = 3 - 3 * h, 3 * h
        if slot == "A2":
            return jnp.where(wraps, ahead, behind)
        return jnp.where(wraps, behind, ahead)

    def near_product(slot, link, m):
        which = weight_of(slot, link)
        count = dict(((a, b), c) for a, b, c in SLOTS)[slot, link]
        first = jnp.where(step[link] == 1, 0, ROUNDS - count) + m
        at = BASE[slot, link] + m
        high = [w_high[which, first + i] for i in range(2)]
        low = [w_low[which, first + i] for i in range(2)]
        left = jnp.concatenate(high + high + low, axis=1)
        for to in (slice(0, cols // 2), slice(cols // 2, cols)):
            value = jnp.concatenate([got[at, :, to], got[at + 1, :, to]], axis=0)
            out[:, to] = out[:, to] + matmul(left, three(value))

    def far_copy(level, k):
        return remote(sent.at[level, k], came.at[level, k], far_send.at[level, k],
                      far_recv.at[level, k], partner(level))

    two_on = chip(0, 4 * odd - 2)

    def first_leg(k):
        i = RELAYED.index(k)
        return remote(sent.at[4, k], mid.at[i], far_send.at[4, k], mid_recv.at[i], two_on)

    def second_leg(k):
        i = RELAYED.index(k)
        return remote(mid.at[i], came.at[4, k], mid_send.at[i], far_recv.at[4, k], two_on)

    here = [pl.ds(wide * k, wide) for k in range(PARTS)]
    waited = set()

    def need(name):
        if name not in waited:
            waited.add(name)
            loads[name].wait()

    def prepare(which):
        need("near")
        if which == OWN:
            scales = None
        else:
            offset = {v: k for k, v in PLUS.items()}[which]
            count = zs * XS
            scales = [
                jnp.where((nb[0, j] - leaf - offset + 2 * count) % count == 0, 1.0, 0.0).astype(F32)
                for j in range(2)
            ]

        def body(i, carry):
            at = pl.ds(pl.multiple_of(i * tall, tall), tall)
            if scales is None:
                value = near[0, at, :]
            else:
                value = scales[0] * near[1, at, :] + scales[1] * near[2, at, :]
            high, low = split(value)
            for c in range(ROUNDS):
                w_high[which, c, at, :] = high[:, tall * c:tall * (c + 1)]
                w_low[which, c, at, :] = low[:, tall * c:tall * (c + 1)]
            return carry

        lax.fori_loop(0, ROUNDS, body, 0)

    for name, args in tokens():
        if name == "own":
            link, m = args[0], int(args[1])
            if link == "P":
                own_copy(link, m).start()
            else:
                @pl.when(end)
                def _():
                    lift_copy(m).start()

                @pl.when(middle)
                def _():
                    own_copy(link, m).start()
        elif name == "comp":
            k = int(args[0])
            if "comp" not in waited:
                need("comp")
                high, low = split(comp[...].T)
                comp3[:, :rows] = high
                comp3[:, rows:2 * rows] = high
                comp3[:, 2 * rows:] = low
                need("x")
            high, low = split(xv[:, here[k]])
            x_high[:, here[k]] = high
            x_low[:, here[k]] = low
            sent[0, k] = matmul(comp3[...], jnp.concatenate([high, low, high], axis=0))
            far_copy(0, k).start()
        elif name == "L":
            level, k = int(args[0]), int(args[1])
            if "trans" not in waited:
                need("trans")
                for i in range(5):
                    for j in range(2):
                        high, low = split(trans[2 * i + j])
                        at = 3 * rank * j
                        trans6[i, :, at:at + rank] = high
                        trans6[i, :, at + rank:at + 2 * rank] = high
                        trans6[i, :, at + 2 * rank:at + 3 * rank] = low
            far_copy(level, k).wait_recv()
            both = jnp.concatenate([three(sent[level, k]), three(came[level, k])], axis=0)
            coeffs = matmul(trans6[level], both)
            if level < 4:
                sent[level + 1, k] = coeffs
                if level == 3 and k in RELAYED:
                    first_leg(k).start()
                else:
                    far_copy(level + 1, k).start()
            else:
                if "expa" not in waited:
                    need("expa")
                    high, low = split(expa[...])
                    expa3[:, :rank] = high
                    expa3[:, rank:2 * rank] = high
                    expa3[:, 2 * rank:] = low
                out[:, here[k]] = out[:, here[k]] + matmul(expa3[...], three(coeffs))
        elif name == "R":
            k = int(args[0])
            first_leg(k).wait_recv()
            second_leg(k).start()
        elif name == "prep":
            prepare(int(args[0]))
        elif name == "ownmm":
            at = slice(cols // 2 * int(args[0]), cols // 2 * (int(args[0]) + 1))
            high = [w_high[OWN, c] for c in range(ROUNDS)]
            low = [w_low[OWN, c] for c in range(ROUNDS)]
            left = jnp.concatenate(high + high + low, axis=1)
            right = jnp.concatenate([x_high[:, at], x_low[:, at], x_high[:, at]], axis=0)
            out[:, at] = matmul(left, right)
        elif name == "Z0":
            m = int(args[0])

            @pl.when(end)
            def _():
                arrived("Z0", "Q", m)
                pass_copy("Z0", "Q", m).start()
        else:
            link, m = args[0], int(args[1])
            arrived(name, link, m)
            if name == "A1":
                pass_copy("A1", link, m).start()
            if name == "A2":
                z_copy(link, m).start()

                @pl.when(end)
                def _():
                    pass_copy("A2", link, m).start()
            if name == "ZR":
                @pl.when(middle)
                def _():
                    pass_copy("ZR", link, m).start()
            if m % 2:
                near_product(name, link, m - 1)

    for link in "PQ":
        for m in range(COUNT[link]):
            own_copy(link, m).wait_send()
            z_copy(link, m).wait_send()
            pass_copy("A2", link, m).wait_send()
        for m in range(COUNT[OTHER[link]]):
            pass_copy("A1", link, m).wait_send()

    @pl.when(end)
    def _():
        for m in range(COUNT["Q"]):
            pass_copy("Z0", "Q", m).wait_send()

    for level in range(5):
        for k in range(PARTS):
            far_copy(level, k).wait_send()
    for k in RELAYED:
        second_leg(k).wait_send()


def per_device(charges, near_blocks, neighbours, compress, transfer, expand):
    rows, cols = charges.shape
    rank = compress.shape[2]
    leaves = lax.axis_size("leaf")
    tall, wide = rows // ROUNDS, cols // PARTS
    anywhere = pl.BlockSpec(memory_space=pl.ANY)
    dma = pltpu.SemaphoreType.DMA
    vmem = pltpu.VMEM
    return pl.pallas_call(
        functools.partial(kernel, leaves // XS),
        out_shape=jax.ShapeDtypeStruct((rows, cols), F32),
        in_specs=[pl.BlockSpec(memory_space=pltpu.SMEM)] + [anywhere] * 5,
        out_specs=pl.BlockSpec(memory_space=pltpu.VMEM),
        scratch_shapes=[
            vmem((rows, cols), F32),
            vmem((rows, cols), BF16),
            vmem((rows, cols), BF16),
            vmem((HOLD, tall, cols), F32),
            vmem((5, ROUNDS, rows, tall), BF16),
            vmem((5, ROUNDS, rows, tall), BF16),
            vmem((3, rows, rows), F32),
            vmem((rows, rank), F32),
            vmem((rank, 3 * rows), BF16),
            vmem((10, rank, rank), F32),
            vmem((5, rank, 6 * rank), BF16),
            vmem((rows, rank), F32),
            vmem((rows, 3 * rank), BF16),
            vmem((5, PARTS, rank, wide), F32),
            vmem((5, PARTS, rank, wide), F32),
            vmem((len(RELAYED), rank, wide), F32),
            dma((5,)),
            dma((HOLD + ROUNDS,)),
            dma((HOLD,)),
            dma((5, PARTS)),
            dma((5, PARTS)),
            dma((len(RELAYED),)),
            dma((len(RELAYED),)),
        ],
        compiler_params=pltpu.CompilerParams(
            collective_id=0, has_side_effects=True, vmem_limit_bytes=63 << 20),
        name="operator",
    )(
        neighbours,
        charges,
        near_blocks[0],
        compress[0],
        transfer[0].reshape(10, rank, rank),
        expand[0],
    )


def solution(mesh):
    in_specs = (
        P("leaf", "rhs"),
        P("leaf", None, None, None),
        P("leaf", None),
        P("leaf", None, None),
        P("leaf", None, None, None, None),
        P("leaf", None, None),
    )
    out_specs = P("leaf", "rhs")
    return jax.shard_map(
        per_device, mesh=mesh, in_specs=in_specs, out_specs=out_specs, check_vma=False
    )
```

time: 287 us -> 177 us (0.62)
  the two profiles are of different devices: /device:TPU:16 before, /device:TPU:22 now
where the time goes in v1:
time: 177 us
  Pallas kernels  169 us (95%)
  local copies, waits for them, and re-layouts  8.39 us (5%)
    pallas_call x1, Pallas kernels, per_device(): pl.pallas_call(functools.partial(kernel, leaves // XS), out_shape=jax.Sha...  169 us
    unnamed x3, local copies, waits for them, and re-layouts  8.39 us

profile of v1, /device:TPU:22, one launch (start us, length us, event | category | flops | bytes accessed | tf_op | source)
XLA Modules:
  0.0 177.0 jit_solution(14665425235012375551)
XLA Ops:
  0.0 2.2 %copy.7 = f32[1,768,192]{2,1,0:T(8,128)} copy(f32[1,768,192]{1,2,0:T(8,128)} %param.9) | data formatting | bytes 1179648 | tf_op args[3]
  2.2 2.2 %copy.8 = f32[1,768,192]{2,1,0:T(8,128)} copy(f32[1,768,192]{1,2,0:T(8,128)} %param.11) | data formatting | bytes 1179648 | tf_op args[5]
  4.4 168.6 %operator.1 = f32[768,1024]{1,0:T(8,128)} custom-call(s32[1,2]{1,0:T(1,128)} %nb.1, f32[768,1024]{1,0:T(8,128)} %x_hbm.1, f32[3,768,768]{2,1,0:T(8,128)} %bitcast.4, f32[768,192]{1,0:T(8,128)} %bitcast.5, f32[10,192,192]{2,1,0:T(8,128)} %bitcast.7, f32[768,192]{1,0:T(8,128)} %bitcast.6), custom_call_target="tpu_custom_call" | custom-call | tf_op jit(solution)/shard_map/operator/pallas_call | solution.py:328
  173.1 4.0 %copy.10 = f32[768,1024]{1,0:T(8,128)} copy(f32[768,1024]{1,0:T(8,128)} %operator.1) | data formatting | bytes 6291456

commit v2 on v1

--- a/solution.py
+++ b/solution.py
@@ -10,10 +10,12 @@
 F32, BF16 = jnp.float32, jnp.bfloat16
 XS = 4
 PARTS = 4
-ROUNDS = 6
-COUNT = {"P": 2, "Q": 4}
-SLOTS = (("A1", "P", 4), ("A1", "Q", 2), ("A2", "P", 2), ("A2", "Q", 4), ("A3", "P", 4),
-         ("A3", "Q", 2), ("ZR", "P", 2), ("ZR", "Q", 4), ("Z0", "Q", 4))
+ROUNDS = 12
+TOGETHER = 4
+LANES = 128
+COUNT = {"P": 4, "Q": 8}
+SLOTS = (("A1", "P", 8), ("A1", "Q", 4), ("A2", "P", 4), ("A2", "Q", 8), ("A3", "P", 8),
+         ("A3", "Q", 4), ("ZR", "P", 4), ("ZR", "Q", 8), ("Z0", "Q", 8))
 BASE, HOLD = {}, 0
 for _slot, _link, _count in SLOTS:
     BASE[_slot, _link] = HOLD
@@ -21,16 +23,20 @@
 OTHER = {"P": "Q", "Q": "P"}
 PLUS = {-2: 0, -1: 1, 1: 2, 2: 3}
 OWN = 4
-RELAYED = (0, 2)
+RELAYED = (0, 2, 3)
 
 ORDER = (
-    "own Q 0", "comp 0", "prep 4", "comp 1", "prep 0", "L 0 0", "L 0 1", "own Q 1", "Z0 0",
-    "prep 2", "comp 3", "comp 2", "L 1 1", "ownmm 0", "L 0 3", "prep 1", "own P 0", "Z0 1",
-    "L 2 1", "L 0 2", "L 1 0", "own Q 2", "L 2 0", "ownmm 1", "prep 3", "L 1 3", "A1 Q 0", "L 3 1",
-    "A1 P 0", "L 2 3", "L 1 2", "own P 1", "Z0 2", "A2 P 0", "A1 P 1", "own Q 3", "L 2 2",
-    "A1 P 2", "A2 Q 0", "Z0 3", "L 3 0", "A1 Q 1", "ZR Q 0", "A2 Q 1", "L 3 2", "ZR P 0", "A2 Q 2",
-    "A1 P 3", "A3 Q 0", "ZR Q 1", "A2 P 1", "R 0", "R 2", "A3 P 0", "A2 Q 3", "ZR Q 2", "A3 P 1",
-    "L 3 3", "ZR P 1", "ZR Q 3", "L 4 2", "A3 P 2", "L 4 1", "L 4 0", "A3 P 3", "A3 Q 1", "L 4 3",
+    "own Q 0", "own Q 1", "comp 0", "prep 4", "comp 1", "L 0 0", "prep 2", "L 0 1", "own Q 2",
+    "comp 3", "Z0 0", "comp 2", "prep 3", "L 1 0", "Z0 1", "own Q 3", "ownmm 1", "L 2 0",
+    "own P 0", "prep 1", "L 1 1", "ownmm 0", "own Q 4", "Z0 2", "prep 0", "own P 1", "A1 Q 0",
+    "L 2 1", "A1 P 0", "L 0 3", "Z0 3", "L 3 0", "A2 P 0", "L 0 2", "A1 Q 1", "own P 2", "A1 P 1",
+    "L 3 1", "Z0 4", "own P 3", "L 1 3", "own Q 5", "A2 Q 0", "L 2 3", "A1 P 2", "A1 P 3",
+    "own Q 6", "A2 P 1", "ZR P 0", "A1 Q 2", "A2 Q 1", "L 1 2", "R 0", "Z0 5", "own Q 7", "ZR Q 0",
+    "A2 P 2", "A1 Q 3", "ZR P 1", "L 4 1", "A2 Q 2", "Z0 6", "A1 P 4", "A2 Q 3", "L 2 2", "A1 P 5",
+    "Z0 7", "L 3 3", "ZR Q 1", "A2 Q 4", "ZR Q 2", "A1 P 6", "ZR Q 3", "A3 P 0", "A2 Q 5", "L 3 2",
+    "ZR P 2", "ZR Q 4", "L 4 0", "A3 Q 0", "A2 Q 6", "A3 P 1", "ZR Q 5", "A1 P 7", "A3 Q 1",
+    "A2 P 3", "R 3", "ZR Q 6", "A3 P 2", "A3 Q 2", "A3 P 3", "A3 P 4", "A2 Q 7", "R 2", "A3 P 5",
+    "ZR P 3", "A3 Q 3", "ZR Q 7", "L 4 3", "A3 P 6", "A3 P 7", "L 4 2",
 )
 
 
@@ -109,7 +115,7 @@
         return x_hbm.at[pl.ds(pl.multiple_of(tall * (first + m), tall), tall)]
 
     def own_copy(link, m):
-        return near_copy(HOLD + m + 4 * (link == "P"), own_rows(link, m), "A1", OTHER[link], m,
+        return near_copy(HOLD + m + COUNT["Q"] * (link == "P"), own_rows(link, m), "A1", OTHER[link], m,
                          chip(step[link], 0))
 
     def lift_copy(m):
@@ -147,13 +153,14 @@
     def near_product(slot, link, m):
         which = weight_of(slot, link)
         count = dict(((a, b), c) for a, b, c in SLOTS)[slot, link]
-        first = jnp.where(step[link] == 1, 0, ROUNDS - count) + m
+        first = (jnp.where(step[link] == 1, 0, ROUNDS - count) + m) * tall // LANES
         at = BASE[slot, link] + m
-        high = [w_high[which, first + i] for i in range(2)]
-        low = [w_low[which, first + i] for i in range(2)]
+        pieces = TOGETHER * tall // LANES
+        high = [w_high[which, first + i] for i in range(pieces)]
+        low = [w_low[which, first + i] for i in range(pieces)]
         left = jnp.concatenate(high + high + low, axis=1)
         for to in (slice(0, cols // 2), slice(cols // 2, cols)):
-            value = jnp.concatenate([got[at, :, to], got[at + 1, :, to]], axis=0)
+            value = jnp.concatenate([got[at + i, :, to] for i in range(TOGETHER)], axis=0)
             out[:, to] = out[:, to] + matmul(left, three(value))
 
     def far_copy(level, k):
@@ -191,18 +198,18 @@
             ]
 
         def body(i, carry):
-            at = pl.ds(pl.multiple_of(i * tall, tall), tall)
+            at = pl.ds(pl.multiple_of(i * LANES, LANES), LANES)
             if scales is None:
                 value = near[0, at, :]
             else:
                 value = scales[0] * near[1, at, :] + scales[1] * near[2, at, :]
             high, low = split(value)
-            for c in range(ROUNDS):
-                w_high[which, c, at, :] = high[:, tall * c:tall * (c + 1)]
-                w_low[which, c, at, :] = low[:, tall * c:tall * (c + 1)]
+            for c in range(rows // LANES):
+                w_high[which, c, at, :] = high[:, LANES * c:LANES * (c + 1)]
+                w_low[which, c, at, :] = low[:, LANES * c:LANES * (c + 1)]
             return carry
 
-        lax.fori_loop(0, ROUNDS, body, 0)
+        lax.fori_loop(0, rows // LANES, body, 0)
 
     for name, args in tokens():
         if name == "own":
@@ -221,7 +228,7 @@
             k = int(args[0])
             if "comp" not in waited:
                 need("comp")
-                high, low = split(comp[...].T)
+                high, low = split(comp[...])
                 comp3[:, :rows] = high
                 comp3[:, rows:2 * rows] = high
                 comp3[:, 2 * rows:] = low
@@ -254,7 +261,7 @@
             else:
                 if "expa" not in waited:
                     need("expa")
-                    high, low = split(expa[...])
+                    high, low = split(expa[...].T)
                     expa3[:, :rank] = high
                     expa3[:, rank:2 * rank] = high
                     expa3[:, 2 * rank:] = low
@@ -267,8 +274,8 @@
             prepare(int(args[0]))
         elif name == "ownmm":
             at = slice(cols // 2 * int(args[0]), cols // 2 * (int(args[0]) + 1))
-            high = [w_high[OWN, c] for c in range(ROUNDS)]
-            low = [w_low[OWN, c] for c in range(ROUNDS)]
+            high = [w_high[OWN, c] for c in range(rows // LANES)]
+            low = [w_low[OWN, c] for c in range(rows // LANES)]
             left = jnp.concatenate(high + high + low, axis=1)
             right = jnp.concatenate([x_high[:, at], x_low[:, at], x_high[:, at]], axis=0)
             out[:, at] = matmul(left, right)
@@ -294,8 +301,8 @@
                 @pl.when(middle)
                 def _():
                     pass_copy("ZR", link, m).start()
-            if m % 2:
-                near_product(name, link, m - 1)
+            if (m + 1) % TOGETHER == 0:
+                near_product(name, link, m + 1 - TOGETHER)
 
     for link in "PQ":
         for m in range(COUNT[link]):
@@ -335,14 +342,14 @@
             vmem((rows, cols), BF16),
             vmem((rows, cols), BF16),
             vmem((HOLD, tall, cols), F32),
-            vmem((5, ROUNDS, rows, tall), BF16),
-            vmem((5, ROUNDS, rows, tall), BF16),
+            vmem((5, rows // LANES, rows, LANES), BF16),
+            vmem((5, rows // LANES, rows, LANES), BF16),
             vmem((3, rows, rows), F32),
-            vmem((rows, rank), F32),
+            vmem((rank, rows), F32),
             vmem((rank, 3 * rows), BF16),
             vmem((10, rank, rank), F32),
             vmem((5, rank, 6 * rank), BF16),
-            vmem((rows, rank), F32),
+            vmem((rank, rows), F32),
             vmem((rows, 3 * rank), BF16),
             vmem((5, PARTS, rank, wide), F32),
             vmem((5, PARTS, rank, wide), F32),
@@ -362,9 +369,9 @@
         neighbours,
         charges,
         near_blocks[0],
-        compress[0],
+        compress[0].T,
         transfer[0].reshape(10, rank, rank),
-        expand[0],
+        expand[0].T,
     )
 
 

time: 177 us -> 160 us (0.904)
  the two profiles are of different devices: /device:TPU:22 before, /device:TPU:16 now
where the time goes in v2:
time: 160 us
  Pallas kernels  156 us (98%)
  local copies, waits for them, and re-layouts  3.97 us (2%)
    pallas_call x1, Pallas kernels, per_device(): pl.pallas_call(functools.partial(kernel, leaves // XS), out_shape=jax.Sha...  156 us
    unnamed x1, local copies, waits for them, and re-layouts  3.97 us

profile of v2, /device:TPU:16, one launch (start us, length us, event | category | flops | bytes accessed | tf_op | source)
XLA Modules:
  0.0 159.8 jit_solution(2315028020122527998)
XLA Ops:
  0.0 155.9 %operator.1 = f32[768,1024]{1,0:T(8,128)} custom-call(s32[1,2]{1,0:T(1,128)} %nb.1, f32[768,1024]{1,0:T(8,128)} %x_hbm.1, f32[3,768,768]{2,1,0:T(8,128)} %bitcast.8, f32[192,768]{1,0:T(8,128)} %bitcast.10, f32[10,192,192]{2,1,0:T(8,128)} %bitcast.9, f32[192,768]{1,0:T(8,128)} %bitcast.11), custom_call_target="tpu_custom_call" | custom-call | tf_op jit(solution)/shard_map/operator/pallas_call | solution.py:335
  155.9 4.0 %copy.8 = f32[768,1024]{1,0:T(8,128)} copy(f32[768,1024]{1,0:T(8,128)} %operator.1) | data formatting | bytes 6291456

commit v3 on v2

--- a/solution.py
+++ b/solution.py
@@ -26,17 +26,17 @@
 RELAYED = (0, 2, 3)
 
 ORDER = (
-    "own Q 0", "own Q 1", "comp 0", "prep 4", "comp 1", "L 0 0", "prep 2", "L 0 1", "own Q 2",
-    "comp 3", "Z0 0", "comp 2", "prep 3", "L 1 0", "Z0 1", "own Q 3", "ownmm 1", "L 2 0",
-    "own P 0", "prep 1", "L 1 1", "ownmm 0", "own Q 4", "Z0 2", "prep 0", "own P 1", "A1 Q 0",
-    "L 2 1", "A1 P 0", "L 0 3", "Z0 3", "L 3 0", "A2 P 0", "L 0 2", "A1 Q 1", "own P 2", "A1 P 1",
-    "L 3 1", "Z0 4", "own P 3", "L 1 3", "own Q 5", "A2 Q 0", "L 2 3", "A1 P 2", "A1 P 3",
-    "own Q 6", "A2 P 1", "ZR P 0", "A1 Q 2", "A2 Q 1", "L 1 2", "R 0", "Z0 5", "own Q 7", "ZR Q 0",
-    "A2 P 2", "A1 Q 3", "ZR P 1", "L 4 1", "A2 Q 2", "Z0 6", "A1 P 4", "A2 Q 3", "L 2 2", "A1 P 5",
-    "Z0 7", "L 3 3", "ZR Q 1", "A2 Q 4", "ZR Q 2", "A1 P 6", "ZR Q 3", "A3 P 0", "A2 Q 5", "L 3 2",
-    "ZR P 2", "ZR Q 4", "L 4 0", "A3 Q 0", "A2 Q 6", "A3 P 1", "ZR Q 5", "A1 P 7", "A3 Q 1",
-    "A2 P 3", "R 3", "ZR Q 6", "A3 P 2", "A3 Q 2", "A3 P 3", "A3 P 4", "A2 Q 7", "R 2", "A3 P 5",
-    "ZR P 3", "A3 Q 3", "ZR Q 7", "L 4 3", "A3 P 6", "A3 P 7", "L 4 2",
+    "own Q 0", "comp 0", "comp 1", "own Q 1", "prep 2", "L 0 0", "comp 3", "Z0 0", "prep 4",
+    "prep 1", "L 0 1", "own P 0", "own Q 2", "Z0 1", "L 1 0", "comp 2", "own Q 3", "Z0 2", "L 2 0",
+    "ownmm 0", "L 1 1", "L 0 3", "prep 3", "ownmm 1", "A1 Q 0", "own Q 4", "own P 1", "A1 P 0",
+    "A1 P 1", "L 2 1", "L 1 3", "L 3 0", "Z0 3", "prep 0", "A2 P 0", "own Q 5", "A2 Q 0", "L 0 2",
+    "own Q 6", "L 2 3", "A1 Q 1", "L 3 1", "own P 2", "A1 P 2", "own P 3", "Z0 4", "ZR P 0",
+    "A1 P 3", "A2 P 1", "Z0 5", "A1 Q 2", "L 1 2", "ZR Q 0", "A2 Q 1", "A1 P 4", "Z0 6", "A2 P 2",
+    "own Q 7", "A3 Q 0", "A2 Q 2", "L 2 2", "A1 Q 3", "ZR Q 1", "L 3 3", "A1 P 5", "R 0", "ZR P 1",
+    "A3 P 0", "A1 P 6", "Z0 7", "A3 P 1", "ZR Q 2", "A2 Q 3", "A2 P 3", "A2 Q 4", "ZR Q 3",
+    "A3 P 2", "L 3 2", "A1 P 7", "A3 P 3", "A2 Q 5", "ZR P 2", "R 3", "A3 Q 1", "A3 Q 2", "A2 Q 6",
+    "ZR Q 4", "L 4 0", "ZR P 3", "L 4 1", "A3 Q 3", "ZR Q 5", "A2 Q 7", "R 2", "ZR Q 6", "A3 P 4",
+    "A3 P 5", "ZR Q 7", "L 4 3", "A3 P 6", "A3 P 7", "L 4 2",
 )
 
 

time: 160 us -> 159 us (level)
  Pallas kernels: 156 us -> 154 us
    pallas_call x1, Pallas kernels: 156 us -> 154 us  [per_device(): pl.pallas_call(functools.partial(kernel, leaves // XS), out_shape=jax.Sha...]
where the time goes in v3:
time: 159 us; the launch traced here: 158 us
  Pallas kernels  154 us (97%)
  local copies, waits for them, and re-layouts  3.97 us (2%)
    pallas_call x1, Pallas kernels, per_device(): pl.pallas_call(functools.partial(kernel, leaves // XS), out_shape=jax.Sha...  154 us
    unnamed x1, local copies, waits for them, and re-layouts  3.97 us

profile of v3, /device:TPU:16, one launch (start us, length us, event | category | flops | bytes accessed | tf_op | source)
XLA Modules:
  0.0 158.1 jit_solution(18232865572798212621)
XLA Ops:
  0.0 154.2 %operator.1 = f32[768,1024]{1,0:T(8,128)} custom-call(s32[1,2]{1,0:T(1,128)} %nb.1, f32[768,1024]{1,0:T(8,128)} %x_hbm.1, f32[3,768,768]{2,1,0:T(8,128)} %bitcast.8, f32[192,768]{1,0:T(8,128)} %bitcast.10, f32[10,192,192]{2,1,0:T(8,128)} %bitcast.9, f32[192,768]{1,0:T(8,128)} %bitcast.11), custom_call_target="tpu_custom_call" | custom-call | tf_op jit(solution)/shard_map/operator/pallas_call | solution.py:335
  154.2 4.0 %copy.8 = f32[768,1024]{1,0:T(8,128)} copy(f32[768,1024]{1,0:T(8,128)} %operator.1) | data formatting | bytes 6291456

commit v4 on v3

--- a/solution.py
+++ b/solution.py
@@ -21,22 +21,25 @@
     BASE[_slot, _link] = HOLD
     HOLD += _count
 OTHER = {"P": "Q", "Q": "P"}
+SPARE = {"A1": 0, "A2": 1, "A3": 2, "ZR": 3}
+SHARED = 2
 PLUS = {-2: 0, -1: 1, 1: 2, 2: 3}
 OWN = 4
-RELAYED = (0, 2, 3)
+RELAYED = (0, 3)
 
 ORDER = (
-    "own Q 0", "comp 0", "comp 1", "own Q 1", "prep 2", "L 0 0", "comp 3", "Z0 0", "prep 4",
-    "prep 1", "L 0 1", "own P 0", "own Q 2", "Z0 1", "L 1 0", "comp 2", "own Q 3", "Z0 2", "L 2 0",
-    "ownmm 0", "L 1 1", "L 0 3", "prep 3", "ownmm 1", "A1 Q 0", "own Q 4", "own P 1", "A1 P 0",
-    "A1 P 1", "L 2 1", "L 1 3", "L 3 0", "Z0 3", "prep 0", "A2 P 0", "own Q 5", "A2 Q 0", "L 0 2",
-    "own Q 6", "L 2 3", "A1 Q 1", "L 3 1", "own P 2", "A1 P 2", "own P 3", "Z0 4", "ZR P 0",
-    "A1 P 3", "A2 P 1", "Z0 5", "A1 Q 2", "L 1 2", "ZR Q 0", "A2 Q 1", "A1 P 4", "Z0 6", "A2 P 2",
-    "own Q 7", "A3 Q 0", "A2 Q 2", "L 2 2", "A1 Q 3", "ZR Q 1", "L 3 3", "A1 P 5", "R 0", "ZR P 1",
-    "A3 P 0", "A1 P 6", "Z0 7", "A3 P 1", "ZR Q 2", "A2 Q 3", "A2 P 3", "A2 Q 4", "ZR Q 3",
-    "A3 P 2", "L 3 2", "A1 P 7", "A3 P 3", "A2 Q 5", "ZR P 2", "R 3", "A3 Q 1", "A3 Q 2", "A2 Q 6",
-    "ZR Q 4", "L 4 0", "ZR P 3", "L 4 1", "A3 Q 3", "ZR Q 5", "A2 Q 7", "R 2", "ZR Q 6", "A3 P 4",
-    "A3 P 5", "ZR Q 7", "L 4 3", "A3 P 6", "A3 P 7", "L 4 2",
+    "own Q 0", "comp 0", "own Q 1", "Z0 0", "comp 1", "L 0 0", "prep 2", "L 0 1", "Z0 1", "comp 3",
+    "own Q 2", "L 1 0", "comp 2", "prep 4", "own Q 3", "L 1 1", "own Q 4", "prep 1", "Z0 2",
+    "L 2 0", "L 0 3", "own P 0", "ownmm 1", "ownmm 0", "L 2 1", "prep 0", "A1 P 0", "A1 Q 0",
+    "prep 3", "own P 1", "own P 2", "A2 Q 0", "A1 P 1", "Z0 3", "L 1 3", "own P 3", "A2 P 0",
+    "own Q 5", "Z0 4", "own P 4", "ZR Q 0", "L 2 3", "A3 P 0", "L 0 2", "A1 Q 1", "A1 Q 2",
+    "L 3 1", "L 3 0", "A2 Q 1", "A2 P 1", "Z0 5", "ZR P 0", "A1 P 2", "A1 P 3", "L 1 2", "A2 P 2",
+    "ZR Q 1", "A1 Q 3", "A3 P 1", "A2 Q 2", "own Q 6", "L 3 3", "ZR P 1", "A3 Q 0", "A1 P 4",
+    "A1 P 5", "own Q 7", "ZR P 2", "L 2 2", "Z0 6", "A2 Q 3", "R 0", "ZR Q 2", "R 3", "A1 P 6",
+    "A2 Q 4", "Z0 7", "ZR Q 3", "A2 P 3", "L 4 1", "A1 Q 4", "A2 Q 5", "A3 P 2", "A3 P 3",
+    "ZR Q 4", "A1 P 7", "A2 Q 6", "ZR Q 5", "A2 Q 7", "ZR Q 6", "A3 Q 1", "A2 P 4", "ZR P 3",
+    "L 3 2", "A3 P 4", "ZR Q 7", "A3 Q 2", "ZR P 4", "A3 P 5", "L 4 3", "L 4 0", "A3 P 6",
+    "A3 Q 3", "A3 Q 4", "A3 P 7", "L 4 2",
 )
 
 
@@ -62,8 +65,8 @@
 
 def kernel(zs, nb, x_hbm, near_hbm, compress_hbm, transfer_hbm, expand_hbm, out,
            xv, x_high, x_low, got, w_high, w_low, near, comp, comp3, trans, trans6,
-           expa, expa3, sent, came, mid, load_sem, near_send, near_recv, far_send, far_recv,
-           mid_send, mid_recv):
+           expa, expa3, sent, came, mid, spare, load_sem, near_send, near_recv, far_send, far_recv,
+           mid_send, mid_recv, spare_send, spare_recv):
     rows, cols = out.shape
     tall, wide = rows // ROUNDS, cols // PARTS
     rank = comp3.shape[0]
@@ -106,9 +109,31 @@
             src_ref=src, dst_ref=dst, send_sem=send, recv_sem=recv,
             device_id=device, device_id_type=pl.DeviceIdType.MESH)
 
+    counts = {(a, b): c for a, b, c in SLOTS}
+
     def near_copy(send, src, slot, link, m, device):
         at = BASE[slot, link] + m
-        return remote(src, got.at[at], near_send.at[send], near_recv.at[at], device)
+        dst = got.at[at]
+        if counts[slot, link] == COUNT["Q"] and m < SHARED:
+            most = pl.ds(wide, cols - wide)
+            src, dst = src.at[:, most], dst.at[:, most]
+        return remote(src, dst, near_send.at[send], near_recv.at[at], device)
+
+    def spare_copy(send, src, slot, device):
+        at = SPARE[slot]
+        return remote(src, spare.at[at], spare_send.at[send], spare_recv.at[at], device)
+
+    def spare_own():
+        first = tall * jnp.where(step["Q"] == 1, 0, ROUNDS - COUNT["Q"])
+        src = x_hbm.at[pl.ds(pl.multiple_of(first, tall), SHARED * tall), pl.ds(0, wide)]
+        return spare_copy(0, src, "A1", chip(step["P"], 0))
+
+    def spare_pass(slot, link):
+        to, send = ("A2", 1) if slot == "A1" else ("A3", 2)
+        return spare_copy(send, spare.at[SPARE[slot]], to, chip(step[link], 0))
+
+    def spare_z():
+        return spare_copy(3, spare.at[SPARE["A2"]], "ZR", chip(0, z_step("P")))
 
     def own_rows(link, m):
         first = jnp.where(step[link] == 1, 0, ROUNDS - COUNT[link])
@@ -127,16 +152,18 @@
         send = BASE["A3", OTHER[link]] + m if to == "A3" else source
         return near_copy(send, got.at[source], to, OTHER[link], m, chip(step[link], 0))
 
-    def z_copy(link, m):
+    def z_step(link):
         h = jnp.where(step[link] == 1, 0, 1)
         wraps = x == (XS - 1) * h
-        dz = jnp.where(wraps, 1, -1) * step[link]
+        return jnp.where(wraps, 1, -1) * step[link]
+
+    def z_copy(link, m):
         source = BASE["A2", link] + m
-        return near_copy(source, got.at[source], "ZR", link, m, chip(0, dz))
+        return near_copy(source, got.at[source], "ZR", link, m, chip(0, z_step(link)))
 
     def arrived(slot, link, m):
         at = BASE[slot, link] + m
-        remote(got.at[at], got.at[at], near_send.at[at], near_recv.at[at], chip(1, 0)).wait_recv()
+        near_copy(at, got.at[at], slot, link, m, chip(1, 0)).wait_recv()
 
     def weight_of(slot, link):
         h = jnp.where(step[link] == 1, 0, 1)
@@ -152,16 +179,31 @@
 
     def near_product(slot, link, m):
         which = weight_of(slot, link)
-        count = dict(((a, b), c) for a, b, c in SLOTS)[slot, link]
+        count = counts[slot, link]
         first = (jnp.where(step[link] == 1, 0, ROUNDS - count) + m) * tall // LANES
         at = BASE[slot, link] + m
-        pieces = TOGETHER * tall // LANES
-        high = [w_high[which, first + i] for i in range(pieces)]
-        low = [w_low[which, first + i] for i in range(pieces)]
-        left = jnp.concatenate(high + high + low, axis=1)
-        for to in (slice(0, cols // 2), slice(cols // 2, cols)):
-            value = jnp.concatenate([got[at + i, :, to] for i in range(TOGETHER)], axis=0)
+
+        def add(skip, to):
+            pieces = range(skip * tall // LANES, TOGETHER * tall // LANES)
+            high = [w_high[which, first + i] for i in pieces]
+            low = [w_low[which, first + i] for i in pieces]
+            left = jnp.concatenate(high + high + low, axis=1)
+            value = jnp.concatenate([got[at + i, :, to] for i in range(skip, TOGETHER)], axis=0)
             out[:, to] = out[:, to] + matmul(left, three(value))
+
+        if count == COUNT["Q"] and m == 0:
+            add(SHARED, slice(0, wide))
+            add(0, slice(wide, cols // 2))
+        else:
+            add(0, slice(0, cols // 2))
+        add(0, slice(cols // 2, cols))
+
+    def spare_product(slot, link):
+        which = weight_of(slot, link)
+        piece = jnp.where(step[link] == 1, (ROUNDS - COUNT["Q"]) * tall // LANES, 0)
+        high, low = w_high[which, piece], w_low[which, piece]
+        left = jnp.concatenate([high, high, low], axis=1)
+        out[:, :wide] = out[:, :wide] + matmul(left, three(spare[SPARE[slot]]))
 
     def far_copy(level, k):
         return remote(sent.at[level, k], came.at[level, k], far_send.at[level, k],
@@ -214,7 +256,9 @@
     for name, args in tokens():
         if name == "own":
             link, m = args[0], int(args[1])
-            if link == "P":
+            if link == "P" and m == COUNT["P"]:
+                spare_own().start()
+            elif link == "P":
                 own_copy(link, m).start()
             else:
                 @pl.when(end)
@@ -286,6 +330,22 @@
             def _():
                 arrived("Z0", "Q", m)
                 pass_copy("Z0", "Q", m).start()
+        elif int(args[1]) == counts[name, args[0]]:
+            link = args[0]
+            spare_copy(0, spare.at[SPARE[name]], name, chip(1, 0)).wait_recv()
+            if name == "A1":
+                spare_pass("A1", link).start()
+            if name == "A2":
+                spare_z().start()
+
+                @pl.when(end)
+                def _():
+                    spare_pass("A2", link).start()
+            if name == "ZR":
+                @pl.when(middle)
+                def _():
+                    spare_pass("ZR", link).start()
+            spare_product(name, link)
         else:
             link, m = args[0], int(args[1])
             arrived(name, link, m)
@@ -304,6 +364,10 @@
             if (m + 1) % TOGETHER == 0:
                 near_product(name, link, m + 1 - TOGETHER)
 
+    spare_own().wait_send()
+    spare_pass("A1", "Q").wait_send()
+    spare_pass("A2", "P").wait_send()
+    spare_z().wait_send()
     for link in "PQ":
         for m in range(COUNT[link]):
             own_copy(link, m).wait_send()
@@ -354,6 +418,7 @@
             vmem((5, PARTS, rank, wide), F32),
             vmem((5, PARTS, rank, wide), F32),
             vmem((len(RELAYED), rank, wide), F32),
+            vmem((len(SPARE), SHARED * tall, wide), F32),
             dma((5,)),
             dma((HOLD + ROUNDS,)),
             dma((HOLD,)),
@@ -361,6 +426,8 @@
             dma((5, PARTS)),
             dma((len(RELAYED),)),
             dma((len(RELAYED),)),
+            dma((len(SPARE),)),
+            dma((len(SPARE),)),
         ],
         compiler_params=pltpu.CompilerParams(
             collective_id=0, has_side_effects=True, vmem_limit_bytes=63 << 20),

time: 159 us -> 169 us (1.063)
  Pallas kernels: 154 us -> 165 us
    pallas_call x1, Pallas kernels: 154 us -> 165 us  [per_device(): pl.pallas_call(functools.partial(kernel, leaves // XS), out_shape=jax.Sha...]
where the time goes in v4:
time: 169 us
  Pallas kernels  165 us (98%)
  local copies, waits for them, and re-layouts  3.97 us (2%)
    pallas_call x1, Pallas kernels, per_device(): pl.pallas_call(functools.partial(kernel, leaves // XS), out_shape=jax.Sha...  165 us
    unnamed x1, local copies, waits for them, and re-layouts  3.97 us

profile of v4, /device:TPU:16, one launch (start us, length us, event | category | flops | bytes accessed | tf_op | source)
XLA Modules:
  0.0 168.6 jit_solution(1392896761165615231)
XLA Ops:
  0.0 164.6 %operator.1 = f32[768,1024]{1,0:T(8,128)} custom-call(s32[1,2]{1,0:T(1,128)} %nb.1, f32[768,1024]{1,0:T(8,128)} %x_hbm.1, f32[3,768,768]{2,1,0:T(8,128)} %bitcast.8, f32[192,768]{1,0:T(8,128)} %bitcast.10, f32[10,192,192]{2,1,0:T(8,128)} %bitcast.9, f32[192,768]{1,0:T(8,128)} %bitcast.11), custom_call_target="tpu_custom_call" | custom-call | tf_op jit(solution)/shard_map/operator/pallas_call | solution.py:399
  164.6 4.0 %copy.8 = f32[768,1024]{1,0:T(8,128)} copy(f32[768,1024]{1,0:T(8,128)} %operator.1) | data formatting | bytes 6291456
